TPU v7x, 128 devices: a whole 4x4x4 slice. The times are simulated.
128 devices in a mesh: cfg: 2 (over y_hi), group: 16 (over y_lo, x, core), mp: 4 (over z).
Axes of the slice: x: 4, y: 4 (y_hi: 2, y_lo: 2; y = y_hi * 2 + y_lo), z: 4, core: 2. Of those that a mesh axis runs over, the one named last changes fastest.
Arguments:
- latents: float32 [16384, 64], P(('group', 'mp')), may hold values from -0.6 to 0.6
- text_hidden: bfloat16 [2, 8192, 3072], P('cfg', ('group', 'mp')), may hold values from -6 to 6
- w_img_in: bfloat16 [64, 3072], replicated, may hold values from -0.75 to 0.75
- w_img_qkv: bfloat16 [3072, 4608], P(None, 'mp'), may hold values from -1 to 1
- w_txt_kv: bfloat16 [3072, 3072], P(None, 'mp'), may hold values from -0.109375 to 0.109375
- q_gain: float32 [128], replicated, may hold values from 0.25 to 1.75
- k_gain: float32 [128], replicated, may hold values from 0.25 to 1.75
- w_out: bfloat16 [1536, 3072], replicated, may hold values from -1 to 1
- w_final: bfloat16 [3072, 64], replicated, may hold values from -0.109375 to 0.109375
- mod_img: float32 [8, 3, 3072], replicated, may hold values from -3 to 3
- mod_txt: float32 [8, 2, 3072], replicated, may hold values from -3 to 3
- mod_final: float32 [8, 2, 3072], replicated, may hold values from -3 to 3
- guide: float32 [16], replicated, may hold values from 1.5 to 5
- step_size: float32 [8], replicated, may hold values from 0.02 to 0.3
- img_len: int32 [16], replicated, may hold values from 1 to 1024, as said below
- txt_len: int32 [16], replicated, may hold values from 1 to 512, as said below
- split_flag: int32 [2, 16], replicated, may hold values from 0 to 1, as said below
- tstep: int32 [16], replicated, may hold values from 0 to 7
Outputs:
- velocity: float32 [2, 8192, 64], P('cfg', ('group', 'mp'))
- next_latents: float32 [2, 8192, 64], P('cfg', ('group', 'mp'))
Inputs may be any that keep to these rules, and one draw needn't show every extreme that they name: `img_len`: some group has exactly 1024 live image tokens. `txt_len`: some group has exactly 512 live text tokens. `split_flag`: entries [c, 2j] and [c, 2j + 1] are equal; at least one such pair carries 1 and at least one carries 0.
All inputs are finite; a program needn't handle non-finite values.
Results may differ from a plain program's by a relative error of at most 0.035.
Values may be sent and summed in bfloat16 or wider, within the bound.
A program may use at most 192 MiB of HBM per device.

v0:
```python
import jax
import jax.numpy as jnp
from jax import lax
from jax.sharding import PartitionSpec as P

HD = 128


def partner(value, axis, bit):
    mask = 2**bit
    pairs = [(source, source ^ mask) for source in range(lax.axis_size(axis))]
    return lax.ppermute(value, axis, pairs)


def layer_norm(values):
    center = values - jnp.mean(values, -1, keepdims=True)
    spread = jnp.mean(center * center, -1, keepdims=True)
    return center * lax.rsqrt(spread + 1e-06)


def head_norm(values, gain):
    return values * lax.rsqrt(jnp.mean(values * values, -1, keepdims=True) + 1e-06) * gain


def pick_entry(table, index):
    return lax.dynamic_index_in_dim(table, index, 0, keepdims=False)


def local(
    latents,
    text_hidden,
    w_img_in,
    w_img_qkv,
    w_txt_kv,
    q_gain,
    k_gain,
    w_out,
    w_final,
    mod_img,
    mod_txt,
    mod_final,
    guide,
    step_size,
    img_len,
    txt_len,
    split_flag,
    tstep,
):
    group_index = lax.axis_index("group")
    mp_index = lax.axis_index("mp")
    cfg_index = lax.axis_index("cfg")
    mp_count = lax.axis_size("mp")
    mate_index = jnp.bitwise_xor(group_index, 1)
    step_index = pick_entry(tstep, group_index)
    mod_rows = pick_entry(mod_img, step_index)
    text_rows = pick_entry(mod_txt, step_index)
    final_rows = pick_entry(mod_final, step_index)
    shard_rows = latents.shape[0]
    half_rows = shard_rows // 2
    full_img = shard_rows * mp_count
    full_txt = text_hidden.shape[1] * mp_count
    local_heads = w_img_qkv.shape[1] // (3 * HD)
    x_img = jnp.dot(latents.astype(jnp.bfloat16), w_img_in, preferred_element_type=jnp.float32)
    lat_full = lax.all_gather(latents.astype(jnp.bfloat16), "mp", axis=0, tiled=True)
    x_full = jnp.dot(lat_full, w_img_in, preferred_element_type=jnp.float32)
    img_full = (layer_norm(x_full) * (1.0 + mod_rows[1]) + mod_rows[0]).astype(jnp.bfloat16)
    txt_mod = (
        layer_norm(text_hidden[0].astype(jnp.float32)) * (1.0 + text_rows[1]) + text_rows[0]
    ).astype(jnp.bfloat16)
    txt_full = lax.all_gather(txt_mod, "mp", axis=0, tiled=True)
    qkv = jnp.dot(img_full, w_img_qkv, preferred_element_type=jnp.float32).reshape(
        full_img, local_heads, 3, HD
    )
    query = head_norm(qkv[:, :, 0], q_gain).astype(jnp.bfloat16)
    key_img = head_norm(qkv[:, :, 1], k_gain).astype(jnp.bfloat16)
    value_img = qkv[:, :, 2].astype(jnp.bfloat16)
    text_kv = jnp.dot(txt_full, w_txt_kv, preferred_element_type=jnp.float32).reshape(
        full_txt, local_heads, 2, HD
    )
    key_txt = head_norm(text_kv[:, :, 0], k_gain).astype(jnp.bfloat16)
    value_txt = text_kv[:, :, 1].astype(jnp.bfloat16)
    key_rows = jnp.concatenate([key_txt, key_img], axis=0)
    value_rows = jnp.concatenate([value_txt, value_img], axis=0)
    mate_keys, mate_values = partner((key_rows, value_rows), "group", 0)
    spots_txt = jnp.arange(full_txt, dtype=jnp.int32)
    spots_img = jnp.arange(full_img, dtype=jnp.int32)

    def live_rows(index):
        return jnp.concatenate(
            [spots_txt < pick_entry(txt_len, index), spots_img < pick_entry(img_len, index)]
        )

    flagged = pick_entry(pick_entry(split_flag, cfg_index), group_index) == 1
    live = jnp.concatenate([live_rows(group_index), live_rows(mate_index) & flagged])
    all_keys = jnp.concatenate([key_rows, mate_keys], axis=0)
    all_values = jnp.concatenate([value_rows, mate_values], axis=0)
    scores = jnp.einsum(
        "qhe,khe->hqk", query, all_keys, preferred_element_type=jnp.float32
    ) * HD ** (-0.5)
    scores = jnp.where(live[None, None, :], scores, -1e30)
    weights = jnp.exp(scores - jnp.max(scores, -1, keepdims=True))
    probs = (weights / jnp.sum(weights, -1, keepdims=True)).astype(jnp.bfloat16)
    mixed = jnp.einsum(
        "hqk,khe->qhe", probs, all_values, preferred_element_type=jnp.float32
    ).astype(jnp.bfloat16)
    mixed = mixed.reshape(full_img, local_heads * HD)
    mixed = lax.all_to_all(mixed, "mp", split_axis=0, concat_axis=1, tiled=True)
    attended = jnp.dot(mixed, w_out, preferred_element_type=jnp.float32)
    hidden = x_img + mod_rows[2] * attended
    final = (layer_norm(hidden) * (1.0 + final_rows[1]) + final_rows[0]).astype(jnp.bfloat16)
    own_velocity = jnp.dot(final, w_final, preferred_element_type=jnp.float32)
    scale = pick_entry(guide, group_index)
    other_velocity = partner(own_velocity.astype(jnp.bfloat16), "cfg", 0).astype(own_velocity.dtype)
    is_cond = cfg_index == 0
    cond_part = jnp.where(is_cond, own_velocity, other_velocity)
    uncond_part = jnp.where(is_cond, other_velocity, own_velocity)
    guided_all = uncond_part + scale * (cond_part - uncond_part)
    guided = lax.dynamic_slice_in_dim(guided_all, cfg_index * half_rows, half_rows, 0)
    row_place = (
        mp_index * shard_rows + cfg_index * half_rows + jnp.arange(half_rows, dtype=jnp.int32)
    )
    row_live = row_place < pick_entry(img_len, group_index)
    guided = jnp.where(row_live[:, None], guided, 0.0)
    start_rows = lax.dynamic_slice_in_dim(latents, cfg_index * half_rows, half_rows, 0)
    moved = start_rows - pick_entry(step_size, step_index) * guided
    return (guided[None], moved[None])


def solution(mesh):
    placed = (
        P(("group", "mp"), None),
        P("cfg", ("group", "mp"), None),
        P(),
        P(None, "mp"),
        P(None, "mp"),
        P(),
        P(),
        P(),
        P(),
        P(),
        P(),
        P(),
        P(),
        P(),
        P(),
        P(),
        P(),
        P(),
    )
    return jax.shard_map(
        local,
        mesh=mesh,
        in_specs=placed,
        out_specs=(P("cfg", ("group", "mp"), None), P("cfg", ("group", "mp"), None)),
        check_vma=False,
    )
```

profile of v0, /device:TPU:0, one launch (start us, length us, event | category | flops | bytes accessed | tf_op | source)
XLA Modules:
  0.0 161.9 jit_solution(1764503549173147141)
XLA Ops:
  7.2 1.3 dynamic_slice.48
  9.8 1.3 convert_reduce_fusion
  11.2 1.5 fusion.21
  13.3 1.5 dynamic-slice_add_fusion
  14.8 2.4 %fusion.24 = bf16[128,3072]{1,0:T(8,128)(2,1)} fusion(bf16[1,128,3072]{2,1,0:T(8,128)(2,1)} %param.19, f32[3072]{0:T(1024)S(1)} %bitcast.102, f32[3072]{0:T(1024)S(1)} %bitcast.103, f32[128]{0:T(128)S(1)} %add_rsqrt_fusion.5, f32[128]{0:T(128)S(1)} %broadcast_multiply_fusion.2), kind=kLoop, calls=%fused_computation.35 | loop fusion | flops 2359296 | bytes 1598464 | tf_op jit(solution)/shard_map/convert_element_type | solution.py:69
  17.3 0.6 copy-done.4
  17.9 13.3 %all_gather.7 = bf16[1024,64]{0,1:T(8,128)(2,1)S(1)} all-gather(bf16[256,64]{0,1:T(8,128)(2,1)S(1)} %convert_element_type.51), channel_id=1, replica_groups=mesh['cfg'=2,'group'=16,'mp'=4] {'mp'}, dimensions={0}, use_global_device_ids=true | all-gather | bytes 163840 | tf_op jit(solution)/shard_map/all_gather | solution.py:64
  31.1 6.4 %fusion.52 = (f32[1024]{0:T(1024)S(1)}, f32[1024,3072]{1,0:T(8,128)}) fusion(bf16[1024,64]{0,1:T(8,128)(2,1)S(1)} %all_gather.7, bf16[64,3072]{1,0:T(8,128)(2,1)S(1)} %copy-done), kind=kOutput, calls=%fused_computation.95 | convolution fusion | flops 405797888 | bytes 13111296 | tf_op jit(solution)/shard_map/dot_general | solution.py:65
  37.5 6.0 %multiply_reduce_fusion = f32[1024]{0:T(1024)S(1)} fusion(f32[1024,3072]{1,0:T(8,128)} %get-tuple-element.15, f32[1024]{0:T(1024)S(1)} %broadcast_multiply_fusion), kind=kLoop, calls=%fused_computation.10 | loop fusion | flops 9436160 | bytes 12591104 | tf_op jit(solution)/shard_map/reduce_sum | solution.py:17
  43.6 0.9 fusion.41
  44.5 1.0 constant_dynamic-slice_fusion
  45.5 14.3 %fusion.6 = f32[1024,1152]{0,1:T(8,128)S(1)} fusion(bf16[3072,1152]{1,0:T(8,128)(2,1)} %param.21, f32[1024,3072]{1,0:T(8,128)} %get-tuple-element.15, f32[3072]{0:T(1024)S(1)} %bitcast.108, f32[3072]{0:T(1024)S(1)} %bitcast.107, f32[1024]{0:T(1024)S(1)} %add_rsqrt_fusion.3, f32[1024]{0:T(1024)S(1)} %broadcast_multiply_fusion), kind=kOutput, calls=%fused_computation.11 | convolution fusion | flops 7263485952 | bytes 24412160 | tf_op jit(solution)/shard_map/dot_general | solution.py:71
  59.7 2.1 %copy-done.1 = f32[1024,1152]{0,1:T(8,128)} copy-done((f32[1024,1152]{0,1:T(8,128)}, f32[1024,1152]{0,1:T(8,128)S(1)}, u32[]{:S(2)}) %copy-start.1) | copy-done | bytes 4718616
  62.1 0.5 copy.41
  62.6 1.4 fusion.50
  64.0 0.6 iota_compare_fusion.2
  64.6 0.6 iota_compare_fusion
  65.2 0.7 iota_compare_fusion.1
  65.9 0.5 fusion.25
  66.4 1.1 fusion.27
  67.6 7.3 %fusion.56 = f32[512,768]{1,0:T(8,128)} fusion(bf16[512,3072]{1,0:T(8,128)(2,1)} %all-gather.2.cloned.1.call-done, bf16[3072,768]{1,0:T(8,128)(2,1)} %param.22), kind=kOutput, calls=%fused_computation.99 | convolution fusion | flops 2415919104 | bytes 9437184 | tf_op jit(solution)/shard_map/dot_general | solution.py:77
  74.9 2.1 %reshape.127 = f32[512,3,2,128]{3,2,1,0:T(2,128)S(1)} reshape(f32[512,768]{1,0:T(8,128)} %fusion.56) | data formatting | bytes 3145728 | tf_op jit(solution)/shard_map/reshape | solution.py:77
  77.0 0.5 slice.60
  78.2 1.1 pad_maximum_fusion.2
  79.3 0.7 iota_compare_fusion.3
  80.0 0.6 dynamic_slice.54
  81.3 1.6 multiply_reduce_fusion.2
  82.9 0.6 add_rsqrt_fusion.1
  83.5 1.5 fusion.36
  85.0 0.8 slice.57
  85.8 1.0 copy.42
  86.9 0.6 collective-permute-start
  87.5 19.3 %fusion.53 = (f32[3,1024]{1,0:T(4,128)S(1)}, f32[3,1024,3072]{2,1,0:T(8,128)}) fusion(pred[3072]{0:T(1024)(128)(4,1)S(1)} %pad_add_fusion, bf16[1536,3,128]{2,0,1:T(8,128)(2,1)} %collective-permute-done.1, bf16[1024,3,128]{2,0,1:T(8,128)(2,1)} %copy-done.2, bf16[512,3,128]{2,0,1:T(8,128)(2,1)} %copy-done.3, f32[1024,3,3,128]{0,3,2,1:T(8,128)} %bitcast.99, ...), kind=kOutput, calls=%fused_computation.96 | convolution fusion | flops 2461928448 | bytes 41713152 | tf_op jit(solution)/shard_map/sub | solution.py:101
  106.8 14.9 %fusion.32 = bf16[1024,3,128]{0,2,1:T(8,128)(2,1)S(1)} fusion(f32[3,1024,3072]{2,1,0:T(8,128)} %get-tuple-element.17, f32[3,1024]{1,0:T(4,128)S(1)} %get-tuple-element.16, bf16[1536,3,128]{0,2,1:T(8,128)(2,1)} %collective-permute-done, bf16[1024,3,128]{0,2,1:T(8,128)(2,1)S(1)} %fusion.36, bf16[512,3,128]{0,2,1:T(8,128)(2,1)S(1)} %bitcast.101), kind=kOutput, calls=%fused_computation.47 | convolution fusion | flops 2442264576 | bytes 40906752 | tf_op jit(solution)/shard_map/hqk,khe->qhe/dot_general | solution.py:103
  121.7 0.6 all_to_all.14
  122.3 1.0 copy.33
  123.2 4.3 %all-to-all-start = ((bf16[4,256,384]{1,2,0:T(8,128)(2,1)}), bf16[4,256,384]{1,2,0:T(8,128)(2,1)S(1)}, u32[]{:S(2)}, u32[]{:S(2)}) async-start(bf16[4,256,384]{1,2,0:T(8,128)(2,1)} %copy.33), calls=%async_computation | async-start | bytes 1572864 | tf_op jit(solution)/shard_map/all_to_all | solution.py:107
  127.5 12.5 %all-to-all-done = bf16[4,256,384]{1,2,0:T(8,128)(2,1)S(1)} async-done(((bf16[4,256,384]{1,2,0:T(8,128)(2,1)}), bf16[4,256,384]{1,2,0:T(8,128)(2,1)S(1)}, u32[]{:S(2)}, u32[]{:S(2)}) %all-to-all-start) | async-done | bytes 786464 | tf_op jit(solution)/shard_map/all_to_all | solution.py:107
  140.0 5.2 %convolution_multiply_fusion = f32[256,3072]{1,0:T(8,128)S(1)} fusion(bf16[256,1536]{0,1:T(8,128)(2,1)S(1)} %bitcast.95, bf16[1536,3072]{1,0:T(8,128)(2,1)} %param.25, f32[3072]{0:T(1024)S(1)} %bitcast.104), kind=kOutput, calls=%fused_computation.18 | convolution fusion | flops 2416705536 | bytes 13381632 | tf_op jit(solution)/shard_map/dot_general | solution.py:108
  145.2 0.7 fusion.54
  146.0 0.5 multiply_reduce_fusion.1
  146.6 0.3 copy-done.13
  146.9 0.7 fusion.55
  147.7 3.3 %collective-permute-start.2 = (bf16[256,64]{0,1:T(8,128)(2,1)S(1)}, bf16[256,64]{0,1:T(8,128)(2,1)S(1)}, u32[]{:S(2)}, u32[]{:S(2)}) collective-permute-start(bf16[256,64]{0,1:T(8,128)(2,1)S(1)} %get-tuple-element.20), channel_id=1, source_target_pairs={{0,64},{64,0},{1,65},{65,1},{2,66},{66,2},{3,67},{67,3},{4,68},{68... | collective-permute-start | bytes 98312 | tf_op jit(solution)/shard_map/ppermute | solution.py:12
  151.0 0.7 add_compare_fusion
  151.7 0.7 dynamic_slice.59
  152.3 0.6 dynamic_slice.56
  153.2 1.9 %subtract_bitcast_fusion = (f32[1,128,64]{1,2,0:T(8,128)}, f32[1,128,64]{1,2,0:T(8,128)}) fusion(f32[256,64]{0,1:T(8,128)S(1)} %copy-done.7, s32[]{:T(128)S(6)} %select_n.65, f32[]{:T(128)} %bitcast.25, f32[]{:T(128)} %bitcast.23, f32[256,64]{0,1:T(8,128)S(1)} %get-tuple-element.21, bf16[256,64]{0,1:T(8,128)(2,1)S(1)} %collective-permute-done.2, pred[]{:T(512)S(6)} %eq.9, ...), kind=kLoop, calls=%fused_computation.62 | loop fusion | flops 73728 | bytes 147597 | tf_op jit(solution)/shard_map/broadcast_in_dim | solution.py:126
  (51 shorter events, 1.5 us)
Async XLA Ops:
  7.2 24.0 %copy-start = (bf16[64,3072]{1,0:T(8,128)(2,1)S(1)}, bf16[64,3072]{1,0:T(8,128)(2,1)}, u32[]{:S(2)}) copy-start(bf16[64,3072]{1,0:T(8,128)(2,1)} %param.20) | copy-start | bytes 1179652
  7.2 10.0 %copy-start.6 = (f32[256,64]{0,1:T(8,128)S(1)}, f32[256,64]{0,1:T(8,128)}, u32[]{:S(2)}) copy-start(f32[256,64]{0,1:T(8,128)} %param.18) | copy-start | bytes 196612
  7.2 60.4 %all-gather.2.cloned.1.call-start = ((), (), s32[]{:S(2)}) async-start(), calls=%async_computation.1 | async-start | bytes 3932160 | tf_op jit(solution)/shard_map/all_gather | solution.py:70
  17.2 0.6 copy-start.4
  59.7 2.2 %copy-start.1 = (f32[1024,1152]{0,1:T(8,128)}, f32[1024,1152]{0,1:T(8,128)S(1)}, u32[]{:S(2)}) copy-start(f32[1024,1152]{0,1:T(8,128)S(1)} %fusion.6) | copy-start | bytes 14155780
  61.9 0.7 copy-start.10
  67.6 10.6 %copy-start.2 = (bf16[1024,3,128]{2,0,1:T(8,128)(2,1)}, bf16[1024,3,128]{2,0,1:T(8,128)(2,1)S(1)}, u32[]{:S(2)}) copy-start(bf16[1024,3,128]{2,0,1:T(8,128)(2,1)S(1)} %fusion.27) | copy-start | bytes 2359300
  74.9 3.0 %copy-start.11 = (f32[128]{0:T(128)S(1)}, f32[128]{0:T(128)}, u32[]{:S(2)}) copy-start(f32[128]{0:T(128)} %param.24) | copy-start | bytes 1540
  77.0 3.0 %copy-start.12 = (s32[2,16]{1,0:T(2,128)S(1)}, s32[2,16]{1,0:T(2,128)}, u32[]{:S(2)}) copy-start(s32[2,16]{1,0:T(2,128)} %param.34) | copy-start | bytes 388
  78.2 1.2 copy-start.3
  79.3 8.2 %collective-permute-start.1 = (bf16[1536,3,128]{2,0,1:T(8,128)(2,1)}, bf16[1536,3,128]{2,0,1:T(8,128)(2,1)}, u32[]{:S(2)}, u32[]{:S(2)}) collective-permute-start(bf16[1536,3,128]{2,0,1:T(8,128)(2,1)} %pad_maximum_fusion.2), channel_id=1, source_target_pairs={{0,4},{4,0},{8,12},{12,8},{16,20},{20,16},{24,28},{28,24},{32,36},... | collective-permute-start | bytes 3538952 | tf_op jit(solution)/shard_map/ppermute | solution.py:12
  86.9 19.9 %collective-permute-start = (bf16[1536,3,128]{0,2,1:T(8,128)(2,1)S(1)}, bf16[1536,3,128]{0,2,1:T(8,128)(2,1)}, u32[]{:S(2)}, u32[]{:S(2)}) collective-permute-start(bf16[1536,3,128]{0,2,1:T(8,128)(2,1)S(1)} %pad_maximum_fusion.1), channel_id=1, source_target_pairs={{0,4},{4,0},{8,12},{12,8},{16,20},{20,16},{24,28},{28,24},{32,36},... | collective-permute-start | bytes 3538952 | tf_op jit(solution)/shard_map/ppermute | solution.py:12
  123.2 16.7 %all-to-all-start = ((bf16[4,256,384]{1,2,0:T(8,128)(2,1)}), bf16[4,256,384]{1,2,0:T(8,128)(2,1)S(1)}, u32[]{:S(2)}, u32[]{:S(2)}) async-start(bf16[4,256,384]{1,2,0:T(8,128)(2,1)} %copy.33), calls=%async_computation | async-start | bytes 1572864 | tf_op jit(solution)/shard_map/all_to_all | solution.py:107
  140.0 5.2 %copy-start.5 = (bf16[256,64]{0,1:T(8,128)(2,1)S(1)}, bf16[256,64]{0,1:T(8,128)(2,1)}, u32[]{:S(2)}) copy-start(bf16[256,64]{0,1:T(8,128)(2,1)} %copy-done.4) | copy-start | bytes 98308
  145.9 0.7 copy-start.8
  145.9 0.7 copy-start.9
  145.9 1.0 copy-start.13
  145.9 5.7 %copy-start.14 = (f32[8]{0:T(128)S(1)}, f32[8]{0:T(128)}, u32[]{:S(2)}) copy-start(f32[8]{0:T(128)} %param.31) | copy-start | bytes 100
  145.9 6.4 %copy-start.15 = (f32[16]{0:T(128)S(1)}, f32[16]{0:T(128)}, u32[]{:S(2)}) copy-start(f32[16]{0:T(128)} %param.30) | copy-start | bytes 196
  145.9 7.2 %copy-start.7 = (f32[256,64]{0,1:T(8,128)S(1)}, f32[256,64]{0,1:T(8,128)}, u32[]{:S(2)}) copy-start(f32[256,64]{0,1:T(8,128)} %param.18) | copy-start | bytes 196612
  147.7 5.5 %collective-permute-start.2 = (bf16[256,64]{0,1:T(8,128)(2,1)S(1)}, bf16[256,64]{0,1:T(8,128)(2,1)S(1)}, u32[]{:S(2)}, u32[]{:S(2)}) collective-permute-start(bf16[256,64]{0,1:T(8,128)(2,1)S(1)} %get-tuple-element.20), channel_id=1, source_target_pairs={{0,64},{64,0},{1,65},{65,1},{2,66},{66,2},{3,67},{67,3},{4,68},{68... | collective-permute-start | bytes 98312 | tf_op jit(solution)/shard_map/ppermute | solution.py:12
Sparse Core Ops, SparseCore 0:
  17.3 42.2 all-gather.1
where the time goes:
time: 163 us; the launch traced here: 162 us
  matrix products  68.8 us (42%)
  other arithmetic  24.9 us (15%)
  between operations  17.1 us (10%)
  local copies, waits for them, and re-layouts  17 us (10%)
  blocking collectives  13.3 us (8%)
  waiting for transfers between devices  12.8 us (8%)
  starting transfers between devices  8.17 us (5%)
    sub x1, matrix products, local(): weights = jnp.exp(scores - jnp.max(scores, -1, keepdims=True))  19.3 us
    dot_general x1, matrix products, local(): jnp.einsum('hqk,khe->qhe', probs, all_values, preferred_element_type=jnp....  14.9 us
    dot_general x1, matrix products, local(): jnp.dot(img_full, w_img_qkv, preferred_element_type=jnp.float32)  14.3 us
    all_gather x1, blocking collectives, local(): lax.all_gather(latents.astype(jnp.bfloat16), 'mp', axis=0, tiled=True)  13.3 us
    all_to_all x1, waiting for transfers between devices, local(): mixed = lax.all_to_all(mixed, 'mp', split_axis=0, concat_axis=1, tiled=True)  12.5 us
    reduce_sum x3, other arithmetic, layer_norm(): spread = jnp.mean(center * center, -1, keepdims=True)  7.98 us
    dot_general x1, matrix products, local(): jnp.dot(txt_full, w_txt_kv, preferred_element_type=jnp.float32)  7.3 us
    dot_general x1, matrix products, local(): x_full = jnp.dot(lat_full, w_img_in, preferred_element_type=jnp.float32)  6.4 us
  transfers between devices with their start and end apart: 5, of which 2 were waited for; matrix products, arithmetic and copies ran while one was open for 38% of the time, Pallas kernels for 0%

commit v1 on v0

--- a/solution.py
+++ b/solution.py
@@ -61,7 +61,11 @@
     full_txt = text_hidden.shape[1] * mp_count
     local_heads = w_img_qkv.shape[1] // (3 * HD)
     x_img = jnp.dot(latents.astype(jnp.bfloat16), w_img_in, preferred_element_type=jnp.float32)
-    lat_full = lax.all_gather(latents.astype(jnp.bfloat16), "mp", axis=0, tiled=True)
+    block = latents.astype(jnp.bfloat16)
+    size = lax.axis_size("mp")
+    shards = jnp.stack([block for _ in range(size)])
+    shards = lax.all_to_all(shards, "mp", split_axis=0, concat_axis=0)
+    lat_full = jnp.concatenate(shards, axis=0)
     x_full = jnp.dot(lat_full, w_img_in, preferred_element_type=jnp.float32)
     img_full = (layer_norm(x_full) * (1.0 + mod_rows[1]) + mod_rows[0]).astype(jnp.bfloat16)
     txt_mod = (

time: 163 us -> 160 us (0.982)
  blocking collectives: 13.3 us -> 0 us
  waiting for transfers between devices: 12.8 us -> 23.6 us
  matrix products: 68.8 us -> 63.7 us
  starting transfers between devices: 8.17 us -> 12.6 us
  local copies, waits for them, and re-layouts: 17 us -> 20.4 us
  other arithmetic: 24.9 us -> 22 us
    all_gather x1 -> x0, blocking collectives: 13.3 us -> none  [local(): lax.all_gather(latents.astype(jnp.bfloat16), 'mp', axis=0, tiled=True)]
    all_gather x1, waiting for transfers between devices: 0.02 us -> 10.3 us  [local(): txt_full = lax.all_gather(txt_mod, 'mp', axis=0, tiled=True)]
    all_to_all x0 -> x1, starting transfers between devices: none -> 5.39 us  [local(): shards = lax.all_to_all(shards, 'mp', split_axis=0, concat_axis=0)]
    reduce_sum x3, other arithmetic: 7.98 us -> 3.32 us  [layer_norm(): spread = jnp.mean(center * center, -1, keepdims=True)]
    dot_general x1, matrix products: 6.4 us -> 1.91 us  [local(): x_full = jnp.dot(lat_full, w_img_in, preferred_element_type=jnp.float32)]
    unnamed x34 -> x42, local copies, waits for them, and re-layouts: 4.78 us -> 8.37 us
  transfers between devices with their start and end apart: 5 -> 6, of which waited for: 2 -> 3; matrix products, arithmetic and copies ran while one was open for 38% -> 38% of each run, Pallas kernels for 0% -> 0%
where the time goes in v1:
time: 160 us; the launch traced here: 159 us
  matrix products  63.7 us (40%)
  waiting for transfers between devices  23.6 us (15%)
  other arithmetic  22 us (14%)
  local copies, waits for them, and re-layouts  20.4 us (13%)
  between operations  17 us (11%)
  starting transfers between devices  12.6 us (8%)
    sub x1, matrix products, local(): weights = jnp.exp(scores - jnp.max(scores, -1, keepdims=True))  19.3 us
    dot_general x1, matrix products, local(): jnp.einsum('hqk,khe->qhe', probs, all_values, preferred_element_type=jnp....  14.8 us
    dot_general x1, matrix products, local(): jnp.dot(img_full, w_img_qkv, preferred_element_type=jnp.float32)  14 us
    all_to_all x1, waiting for transfers between devices, local(): mixed = lax.all_to_all(mixed, 'mp', split_axis=0, concat_axis=1, tiled=True)  12.7 us
    all_gather x1, waiting for transfers between devices, local(): txt_full = lax.all_gather(txt_mod, 'mp', axis=0, tiled=True)  10.3 us
    unnamed x42, local copies, waits for them, and re-layouts  8.37 us
    dot_general x1, matrix products, local(): jnp.dot(txt_full, w_txt_kv, preferred_element_type=jnp.float32)  7.05 us
    all_to_all x1, starting transfers between devices, local(): shards = lax.all_to_all(shards, 'mp', split_axis=0, concat_axis=0)  5.39 us
  transfers between devices with their start and end apart: 6, of which 3 were waited for; matrix products, arithmetic and copies ran while one was open for 38% of the time, Pallas kernels for 0%

profile of v1, /device:TPU:0, one launch (start us, length us, event | category | flops | bytes accessed | tf_op | source)
XLA Modules:
  0.0 159.4 jit_solution(1150286668375766908)
XLA Ops:
  7.2 0.9 convert_element_type.51
  8.1 0.6 copy-done.5
  8.7 0.7 stack.2
  9.4 5.4 %all-to-all-start = ((bf16[4,256,64]{1,2,0:T(8,128)(2,1)}), bf16[4,256,64]{1,2,0:T(8,128)(2,1)S(1)}, u32[]{:S(2)}, u32[]{:S(2)}) async-start(bf16[4,256,64]{1,2,0:T(8,128)(2,1)} %stack.2), calls=%async_computation | async-start | bytes 262144 | tf_op jit(solution)/shard_map/all_to_all | solution.py:67
  14.8 1.2 dynamic_slice.48
  17.3 1.3 convert_reduce_fusion
  18.6 1.5 fusion.21
  20.8 0.8 dynamic-slice_add_fusion.1
  21.6 2.4 %fusion.24 = bf16[128,3072]{1,0:T(8,128)(2,1)} fusion(bf16[1,128,3072]{2,1,0:T(8,128)(2,1)} %param.19, f32[3072]{0:T(1024)S(1)} %bitcast.108, f32[3072]{0:T(1024)S(1)} %bitcast.107, f32[128]{0:T(128)S(1)} %add_rsqrt_fusion.5, f32[128]{0:T(128)S(1)} %broadcast_multiply_fusion.2), kind=kLoop, calls=%fused_computation.35 | loop fusion | flops 2359296 | bytes 1598464 | tf_op jit(solution)/shard_map/convert_element_type | solution.py:73
  24.1 1.6 dynamic-slice_add_fusion
  25.7 1.0 constant_dynamic-slice_fusion
  26.6 0.7 fusion.50
  27.3 1.2 iota_compare_fusion
  28.5 1.2 iota_compare_fusion.1
  29.7 1.1 iota_compare_fusion.2
  30.9 1.9 %fusion.52 = (f32[1024]{0:T(1024)S(1)}, f32[1024,3072]{1,0:T(8,128)S(1)}) fusion(bf16[1024,64]{0,1:T(8,128)(2,1)S(1)} %bitcast.104, bf16[64,3072]{1,0:T(8,128)(2,1)S(1)} %copy-done), kind=kOutput, calls=%fused_computation.95 | convolution fusion | flops 405797888 | bytes 13111296 | tf_op jit(solution)/shard_map/dot_general | solution.py:69
  32.8 1.4 multiply_reduce_fusion
  34.2 3.6 %copy-done.1 = f32[1024,3072]{1,0:T(8,128)} copy-done((f32[1024,3072]{1,0:T(8,128)}, f32[1024,3072]{1,0:T(8,128)S(1)}, u32[]{:S(2)}) %copy-start.1) | copy-done | bytes 12582936
  37.7 14.0 %fusion.6 = f32[1024,1152]{0,1:T(8,128)S(1)} fusion(bf16[3072,1152]{1,0:T(8,128)(2,1)} %param.21, f32[1024,3072]{1,0:T(8,128)} %copy-done.1, f32[3072]{0:T(1024)S(1)} %bitcast.112, f32[3072]{0:T(1024)S(1)} %bitcast.111, f32[1024]{0:T(1024)S(1)} %add_rsqrt_fusion.3, f32[1024]{0:T(1024)S(1)} %broadcast_multiply_fusion), kind=kOutput, calls=%fused_computation.11 | convolution fusion | flops 7263485952 | bytes 24412160 | tf_op jit(solution)/shard_map/dot_general | solution.py:75
  51.7 2.1 %copy-done.2 = f32[1024,1152]{0,1:T(8,128)} copy-done((f32[1024,1152]{0,1:T(8,128)}, f32[1024,1152]{0,1:T(8,128)S(1)}, u32[]{:S(2)}) %copy-start.2) | copy-done | bytes 4718616
  55.6 10.3 %all-gather.2.cloned.1.call-done = bf16[512,3072]{1,0:T(8,128)(2,1)} async-done(((bf16[128,3072]{1,0:T(8,128)(2,1)}), bf16[512,3072]{1,0:T(8,128)(2,1)}) %all-gather.2.cloned.1.call-update) | async-done | bytes 3145744 | tf_op jit(solution)/shard_map/all_gather | solution.py:74
  65.9 7.0 %fusion.56 = f32[512,768]{1,0:T(8,128)} fusion(bf16[512,3072]{1,0:T(8,128)(2,1)} %all-gather.2.cloned.1.call-done, bf16[3072,768]{1,0:T(8,128)(2,1)} %param.22), kind=kOutput, calls=%fused_computation.99 | convolution fusion | flops 2415919104 | bytes 9437184 | tf_op jit(solution)/shard_map/dot_general | solution.py:81
  72.9 2.1 %reshape.132 = f32[512,3,2,128]{3,2,1,0:T(2,128)S(1)} reshape(f32[512,768]{1,0:T(8,128)} %fusion.56) | data formatting | bytes 3145728 | tf_op jit(solution)/shard_map/reshape | solution.py:81
  75.1 0.5 slice.60
  76.2 1.2 pad_maximum_fusion.2
  77.4 0.6 iota_compare_fusion.3
  78.0 0.6 dynamic_slice.54
  79.2 1.6 multiply_reduce_fusion.2
  80.8 0.6 add_rsqrt_fusion.1
  81.4 1.5 fusion.36
  82.9 0.8 slice.57
  83.8 1.0 copy.61
  84.9 0.6 collective-permute-start
  85.4 19.3 %fusion.53 = (f32[3,1024]{1,0:T(4,128)S(1)}, f32[3,1024,3072]{2,1,0:T(8,128)}) fusion(pred[3072]{0:T(1024)(128)(4,1)S(1)} %pad_add_fusion, bf16[1536,3,128]{2,0,1:T(8,128)(2,1)} %collective-permute-done.1, bf16[1024,3,128]{2,0,1:T(8,128)(2,1)} %copy-done.3, bf16[512,3,128]{2,0,1:T(8,128)(2,1)} %copy-done.4, f32[1024,3,3,128]{0,3,2,1:T(8,128)} %bitcast.101, ...), kind=kOutput, calls=%fused_computation.96 | convolution fusion | flops 2461928448 | bytes 41713152 | tf_op jit(solution)/shard_map/sub | solution.py:105
  104.8 14.8 %fusion.32 = bf16[1024,3,128]{0,2,1:T(8,128)(2,1)S(1)} fusion(f32[3,1024,3072]{2,1,0:T(8,128)} %get-tuple-element.17, f32[3,1024]{1,0:T(4,128)S(1)} %get-tuple-element.16, bf16[1536,3,128]{0,2,1:T(8,128)(2,1)} %collective-permute-done, bf16[1024,3,128]{0,2,1:T(8,128)(2,1)S(1)} %fusion.36, bf16[512,3,128]{0,2,1:T(8,128)(2,1)S(1)} %bitcast.103), kind=kOutput, calls=%fused_computation.47 | convolution fusion | flops 2442264576 | bytes 40906752 | tf_op jit(solution)/shard_map/hqk,khe->qhe/dot_general | solution.py:107
  119.6 0.6 all_to_all.18
  120.2 1.0 copy.52
  121.2 3.5 %all-to-all-start.1 = ((bf16[4,256,384]{1,2,0:T(8,128)(2,1)}), bf16[4,256,384]{1,2,0:T(8,128)(2,1)S(1)}, u32[]{:S(2)}, u32[]{:S(2)}) async-start(bf16[4,256,384]{1,2,0:T(8,128)(2,1)} %copy.52), calls=%async_computation.1 | async-start | bytes 1572864 | tf_op jit(solution)/shard_map/all_to_all | solution.py:111
  124.7 12.7 %all-to-all-done.1 = bf16[4,256,384]{1,2,0:T(8,128)(2,1)S(1)} async-done(((bf16[4,256,384]{1,2,0:T(8,128)(2,1)}), bf16[4,256,384]{1,2,0:T(8,128)(2,1)S(1)}, u32[]{:S(2)}, u32[]{:S(2)}) %all-to-all-start.1) | async-done | bytes 786464 | tf_op jit(solution)/shard_map/all_to_all | solution.py:111
  137.4 5.2 %convolution_multiply_fusion = f32[256,3072]{1,0:T(8,128)S(1)} fusion(bf16[256,1536]{0,1:T(8,128)(2,1)S(1)} %bitcast.97, bf16[1536,3072]{1,0:T(8,128)(2,1)} %param.25, f32[3072]{0:T(1024)S(1)} %bitcast.106), kind=kOutput, calls=%fused_computation.18 | convolution fusion | flops 2416705536 | bytes 13381632 | tf_op jit(solution)/shard_map/dot_general | solution.py:112
  142.7 0.7 fusion.54
  144.4 0.7 fusion.55
  145.1 3.1 %collective-permute-start.2 = (bf16[256,64]{0,1:T(8,128)(2,1)S(1)}, bf16[256,64]{0,1:T(8,128)(2,1)S(1)}, u32[]{:S(2)}, u32[]{:S(2)}) collective-permute-start(bf16[256,64]{0,1:T(8,128)(2,1)S(1)} %get-tuple-element.20), channel_id=1, source_target_pairs={{0,64},{64,0},{1,65},{65,1},{2,66},{66,2},{3,67},{67,3},{4,68},{68... | collective-permute-start | bytes 98312 | tf_op jit(solution)/shard_map/ppermute | solution.py:12
  148.2 0.6 add_compare_fusion
  148.9 0.7 dynamic_slice.59
  149.5 0.6 dynamic_slice.56
  150.1 0.5 collective-permute-done.2
  150.6 1.9 %subtract_bitcast_fusion = (f32[1,128,64]{1,2,0:T(8,128)}, f32[1,128,64]{1,2,0:T(8,128)}) fusion(f32[256,64]{0,1:T(8,128)S(1)} %copy-done.7, s32[]{:T(128)S(6)} %select_n.65, f32[]{:T(128)} %bitcast.25, f32[]{:T(128)} %bitcast.23, f32[256,64]{0,1:T(8,128)S(1)} %get-tuple-element.21, bf16[256,64]{0,1:T(8,128)(2,1)S(1)} %collective-permute-done.2, pred[]{:T(512)S(6)} %eq.9, ...), kind=kLoop, calls=%fused_computation.62 | loop fusion | flops 73728 | bytes 147597 | tf_op jit(solution)/shard_map/broadcast_in_dim | solution.py:130
  (62 shorter events, 3.4 us)
Async XLA Ops:
  7.2 23.7 %copy-start = (bf16[64,3072]{1,0:T(8,128)(2,1)S(1)}, bf16[64,3072]{1,0:T(8,128)(2,1)}, u32[]{:S(2)}) copy-start(bf16[64,3072]{1,0:T(8,128)(2,1)} %param.20) | copy-start | bytes 1179652
  7.2 19.4 %copy-start.11 = (s32[16]{0:T(128)S(1)}, s32[16]{0:T(128)}, u32[]{:S(2)}) copy-start(s32[16]{0:T(128)} %param.32) | copy-start | bytes 196
  7.2 19.4 %copy-start.10 = (s32[16]{0:T(128)S(1)}, s32[16]{0:T(128)}, u32[]{:S(2)}) copy-start(s32[16]{0:T(128)} %param.33) | copy-start | bytes 196
  8.1 0.6 copy-start.5
  9.4 21.5 %all-to-all-start = ((bf16[4,256,64]{1,2,0:T(8,128)(2,1)}), bf16[4,256,64]{1,2,0:T(8,128)(2,1)S(1)}, u32[]{:S(2)}, u32[]{:S(2)}) async-start(bf16[4,256,64]{1,2,0:T(8,128)(2,1)} %stack.2), calls=%async_computation | async-start | bytes 262144 | tf_op jit(solution)/shard_map/all_to_all | solution.py:67
  14.8 51.1 %all-gather.2.cloned.1.call-start = ((), (), s32[]{:S(2)}) async-start(), calls=%async_computation.2 | async-start | bytes 3932160 | tf_op jit(solution)/shard_map/all_gather | solution.py:74
  32.8 5.0 %copy-start.1 = (f32[1024,3072]{1,0:T(8,128)}, f32[1024,3072]{1,0:T(8,128)S(1)}, u32[]{:S(2)}) copy-start(f32[1024,3072]{1,0:T(8,128)S(1)} %get-tuple-element.15) | copy-start | bytes 37748740
  51.7 2.2 %copy-start.2 = (f32[1024,1152]{0,1:T(8,128)}, f32[1024,1152]{0,1:T(8,128)S(1)}, u32[]{:S(2)}) copy-start(f32[1024,1152]{0,1:T(8,128)S(1)} %fusion.6) | copy-start | bytes 14155780
  54.1 1.0 copy-start.12
  55.5 20.6 %copy-start.3 = (bf16[1024,3,128]{2,0,1:T(8,128)(2,1)}, bf16[1024,3,128]{2,0,1:T(8,128)(2,1)S(1)}, u32[]{:S(2)}) copy-start(bf16[1024,3,128]{2,0,1:T(8,128)(2,1)S(1)} %fusion.27) | copy-start | bytes 2359300
  75.0 3.0 %copy-start.16 = (s32[2,16]{1,0:T(2,128)S(1)}, s32[2,16]{1,0:T(2,128)}, u32[]{:S(2)}) copy-start(s32[2,16]{1,0:T(2,128)} %param.34) | copy-start | bytes 388
  75.0 4.1 %copy-start.14 = (pred[1024]{0:T(1024)(128)(4,1)S(1)}, pred[1024]{0:T(1024)(128)(4,1)}, u32[]{:S(2)}) copy-start(pred[1024]{0:T(1024)(128)(4,1)} %iota_compare_fusion) | copy-start | bytes 3076
  75.0 4.1 %copy-start.15 = (pred[512]{0:T(512)(128)(4,1)S(1)}, pred[512]{0:T(512)(128)(4,1)}, u32[]{:S(2)}) copy-start(pred[512]{0:T(512)(128)(4,1)} %iota_compare_fusion.2) | copy-start | bytes 1540
  75.0 4.2 %copy-start.13 = (pred[1024]{0:T(1024)(128)(4,1)S(1)}, pred[1024]{0:T(1024)(128)(4,1)}, u32[]{:S(2)}) copy-start(pred[1024]{0:T(1024)(128)(4,1)} %iota_compare_fusion.1) | copy-start | bytes 3076
  76.2 1.2 copy-start.4
  77.4 8.1 %collective-permute-start.1 = (bf16[1536,3,128]{2,0,1:T(8,128)(2,1)}, bf16[1536,3,128]{2,0,1:T(8,128)(2,1)}, u32[]{:S(2)}, u32[]{:S(2)}) collective-permute-start(bf16[1536,3,128]{2,0,1:T(8,128)(2,1)} %pad_maximum_fusion.2), channel_id=1, source_target_pairs={{0,4},{4,0},{8,12},{12,8},{16,20},{20,16},{24,28},{28,24},{32,36},... | collective-permute-start | bytes 3538952 | tf_op jit(solution)/shard_map/ppermute | solution.py:12
  84.9 19.9 %collective-permute-start = (bf16[1536,3,128]{0,2,1:T(8,128)(2,1)S(1)}, bf16[1536,3,128]{0,2,1:T(8,128)(2,1)}, u32[]{:S(2)}, u32[]{:S(2)}) collective-permute-start(bf16[1536,3,128]{0,2,1:T(8,128)(2,1)S(1)} %pad_maximum_fusion.1), channel_id=1, source_target_pairs={{0,4},{4,0},{8,12},{12,8},{16,20},{20,16},{24,28},{28,24},{32,36},... | collective-permute-start | bytes 3538952 | tf_op jit(solution)/shard_map/ppermute | solution.py:12
  121.2 16.2 %all-to-all-start.1 = ((bf16[4,256,384]{1,2,0:T(8,128)(2,1)}), bf16[4,256,384]{1,2,0:T(8,128)(2,1)S(1)}, u32[]{:S(2)}, u32[]{:S(2)}) async-start(bf16[4,256,384]{1,2,0:T(8,128)(2,1)} %copy.52), calls=%async_computation.1 | async-start | bytes 1572864 | tf_op jit(solution)/shard_map/all_to_all | solution.py:111
  137.4 5.2 %copy-start.6 = (bf16[256,64]{0,1:T(8,128)(2,1)S(1)}, bf16[256,64]{0,1:T(8,128)(2,1)}, u32[]{:S(2)}) copy-start(bf16[256,64]{0,1:T(8,128)(2,1)} %copy-done.5) | copy-start | bytes 98308
  143.3 0.7 copy-start.8
  143.3 0.7 copy-start.9
  143.3 1.0 copy-start.17
  143.4 5.5 %copy-start.18 = (f32[8]{0:T(128)S(1)}, f32[8]{0:T(128)}, u32[]{:S(2)}) copy-start(f32[8]{0:T(128)} %param.31) | copy-start | bytes 100
  143.4 6.2 %copy-start.19 = (f32[16]{0:T(128)S(1)}, f32[16]{0:T(128)}, u32[]{:S(2)}) copy-start(f32[16]{0:T(128)} %param.30) | copy-start | bytes 196
  143.4 7.2 %copy-start.7 = (f32[256,64]{0,1:T(8,128)S(1)}, f32[256,64]{0,1:T(8,128)}, u32[]{:S(2)}) copy-start(f32[256,64]{0,1:T(8,128)} %param.18) | copy-start | bytes 196612
  145.1 5.5 %collective-permute-start.2 = (bf16[256,64]{0,1:T(8,128)(2,1)S(1)}, bf16[256,64]{0,1:T(8,128)(2,1)S(1)}, u32[]{:S(2)}, u32[]{:S(2)}) collective-permute-start(bf16[256,64]{0,1:T(8,128)(2,1)S(1)} %get-tuple-element.20), channel_id=1, source_target_pairs={{0,64},{64,0},{1,65},{65,1},{2,66},{66,2},{3,67},{67,3},{4,68},{68... | collective-permute-start | bytes 98312 | tf_op jit(solution)/shard_map/ppermute | solution.py:12
Sparse Core Ops, SparseCore 0:
  24.2 41.6 all-gather.1
